TPU v7x, 32 devices: a whole 2x2x4 slice. The times are simulated.
32 devices in a mesh: rep: 4 (over y, core), ep: 8 (over z, x).
Axes of the slice: x: 2, y: 2, z: 4, core: 2. Of those that a mesh axis runs over, the one named last changes fastest.
Arguments:
- tokens: bfloat16 [4096, 1024], P(('rep', 'ep')), may hold values from -6 to 6
- expert_ids: int32 [4096, 8], P(('rep', 'ep')), may hold values from 0 to 15, all different within a row; in each aligned block of 128 rows (0 to 127, 128 to 255, ...) at most 96 rows name the same one
- route_weights: float32 [4096, 8], P(('rep', 'ep')), may hold values from 0.03 to 0.5
- out_grad: bfloat16 [4096, 1024], P(('rep', 'ep')), may hold values from -4 to 4
- gate_weight: bfloat16 [16, 1024, 384], P('ep'), may hold values from -0.1875 to 0.1875
- up_weight: bfloat16 [16, 1024, 384], P('ep'), may hold values from -0.1875 to 0.1875
- down_weight: bfloat16 [16, 384, 1024], P('ep'), may hold values from -0.3125 to 0.3125
Outputs:
- layer_out: bfloat16 [4096, 1024], P(('rep', 'ep'))
- token_grad: bfloat16 [4096, 1024], P(('rep', 'ep'))
- route_grad: float32 [4096, 8], P(('rep', 'ep'))
- gate_weight_grad: float32 [16, 1024, 384], P('ep', 'rep')
- up_weight_grad: float32 [16, 1024, 384], P('ep', 'rep')
- down_weight_grad: float32 [16, 384, 1024], P('ep', 'rep')
Inputs may be any that keep to these rules, and one draw needn't show every extreme that they name: `expert_ids`: each row names 8 different experts. Among the rows of one device (an aligned block of 128 rows) no expert is named more than 96 times, and in every draw some expert is named exactly 96 times by the rows of some device.
All inputs are finite; a program needn't handle non-finite values.
Results may differ from a plain program's by a relative error of at most 0.014.
Values may be sent and summed in bfloat16 or wider, within the bound.
No kernel may reach another device: no remote copies, remote signals or barrier semaphores. Data moves between devices by JAX's collectives and lax.ppermute only.
A program may use at most 128 MiB of HBM per device.

v0:
```python
import jax
import jax.numpy as jnp
from jax import lax
from jax.sharding import PartitionSpec as P


def silu_parts(gate_pre):
    sigmoid_gate = jax.nn.sigmoid(gate_pre)
    return (gate_pre * sigmoid_gate, sigmoid_gate * (1.0 + gate_pre * (1.0 - sigmoid_gate)))


def expert_forward(expert_in, gate_weight, up_weight, down_weight):
    gate_pre = jnp.einsum(
        "esnd,edf->esnf", expert_in, gate_weight, preferred_element_type=jnp.float32
    )
    up_pre = jnp.einsum("esnd,edf->esnf", expert_in, up_weight, preferred_element_type=jnp.float32)
    silu_gate, silu_slope = silu_parts(gate_pre)
    hidden = (silu_gate * up_pre).astype(jnp.bfloat16)
    expert_out = jnp.einsum(
        "esnf,efd->esnd", hidden, down_weight, preferred_element_type=jnp.float32
    ).astype(jnp.bfloat16)
    return (gate_pre, up_pre, hidden, expert_out)


def expert_backward(out_rows, gate_pre, up_pre, gate_weight, up_weight, down_weight):
    hidden_grad = jnp.einsum(
        "esnd,efd->esnf", out_rows, down_weight, preferred_element_type=jnp.float32
    )
    silu_gate, silu_slope = silu_parts(gate_pre)
    gate_delta = (hidden_grad * up_pre * silu_slope).astype(jnp.bfloat16)
    up_delta = (hidden_grad * silu_gate).astype(jnp.bfloat16)
    in_grads = jnp.einsum(
        "esnf,edf->esnd", gate_delta, gate_weight, preferred_element_type=jnp.float32
    ) + jnp.einsum("esnf,edf->esnd", up_delta, up_weight, preferred_element_type=jnp.float32)
    return (gate_delta, up_delta, in_grads.astype(jnp.bfloat16))


def per_device(tokens, expert_ids, route_weights, out_grad, gate_weight, up_weight, down_weight):
    tok_rows, model_width = tokens.shape
    top_count = expert_ids.shape[1]
    local_experts = gate_weight.shape[0]
    peer_count = lax.axis_size("ep")
    experts = local_experts * peer_count
    capacity = 3 * tok_rows * top_count // (2 * experts)
    slot_total = local_experts * peer_count * capacity
    flat_ids = expert_ids.reshape(-1)
    columns = jnp.arange(experts, dtype=jnp.int32)
    onehot = (flat_ids[:, None] == columns[None, :]).astype(jnp.int32)
    slot_rank = jnp.sum((jnp.cumsum(onehot, axis=0) - 1) * onehot, axis=1)
    target = (
        flat_ids % local_experts * peer_count + flat_ids // local_experts
    ) * capacity + slot_rank
    source = jnp.arange(tok_rows * top_count, dtype=jnp.int32) // top_count

    def pack_rows(pair_rows):
        filled = jnp.zeros((slot_total, model_width), jnp.bfloat16).at[target].set(pair_rows)
        return filled.reshape(local_experts, peer_count, capacity, model_width)

    def unpack_rows(returned):
        return returned.reshape(slot_total, model_width)[target].reshape(
            tok_rows, top_count, model_width
        )

    sent_tokens = pack_rows(tokens[source])
    scaled = (route_weights[:, :, None] * out_grad[:, None, :]).astype(jnp.bfloat16)
    sent_grads = pack_rows(scaled.reshape(tok_rows * top_count, model_width))
    expert_in = lax.all_to_all(sent_tokens, "ep", split_axis=1, concat_axis=1, tiled=True)
    gate_pre, up_pre, hidden, expert_out = expert_forward(
        expert_in, gate_weight, up_weight, down_weight
    )
    returned = lax.all_to_all(expert_out, "ep", split_axis=1, concat_axis=1, tiled=True)
    returned, expert_in, gate_pre, up_pre, hidden = (returned, expert_in, gate_pre, up_pre, hidden)
    out_rows = lax.all_to_all(sent_grads, "ep", split_axis=1, concat_axis=1, tiled=True)
    gate_delta, up_delta, in_grads = expert_backward(
        out_rows, gate_pre, up_pre, gate_weight, up_weight, down_weight
    )
    in_returned = lax.all_to_all(in_grads, "ep", split_axis=1, concat_axis=1, tiled=True)
    grad_down = jnp.einsum("esnf,esnd->efd", hidden, out_rows, preferred_element_type=jnp.float32)
    grad_gate = jnp.einsum(
        "esnd,esnf->edf", expert_in, gate_delta, preferred_element_type=jnp.float32
    )
    grad_up = jnp.einsum("esnd,esnf->edf", expert_in, up_delta, preferred_element_type=jnp.float32)
    down_share = lax.psum_scatter(
        grad_down.astype(jnp.bfloat16), "rep", scatter_dimension=1, tiled=True
    ).astype(jnp.float32)
    gate_share, up_share = (
        lax.psum_scatter(
            grad_gate.astype(jnp.bfloat16), "rep", scatter_dimension=1, tiled=True
        ).astype(jnp.float32),
        lax.psum_scatter(
            grad_up.astype(jnp.bfloat16), "rep", scatter_dimension=1, tiled=True
        ).astype(jnp.float32),
    )
    out_pairs = unpack_rows(returned)
    layer_out = jnp.sum(route_weights[:, :, None] * out_pairs, axis=1).astype(jnp.bfloat16)
    route_grad = jnp.einsum("td,tkd->tk", out_grad, out_pairs, preferred_element_type=jnp.float32)
    token_grad = jnp.sum(unpack_rows(in_returned).astype(jnp.float32), axis=1).astype(jnp.bfloat16)
    return (layer_out, token_grad, route_grad, gate_share, up_share, down_share)


def solution(mesh):
    return jax.shard_map(
        per_device,
        mesh=mesh,
        in_specs=(
            P(("rep", "ep"), None),
            P(("rep", "ep"), None),
            P(("rep", "ep"), None),
            P(("rep", "ep"), None),
            P("ep", None, None),
            P("ep", None, None),
            P("ep", None, None),
        ),
        out_specs=(
            P(("rep", "ep"), None),
            P(("rep", "ep"), None),
            P(("rep", "ep"), None),
            P("ep", "rep", None),
            P("ep", "rep", None),
            P("ep", "rep", None),
        ),
        check_vma=False,
    )
```

profile of v0, /device:TPU:0, one launch (start us, length us, event | category | flops | bytes accessed | tf_op | source)
XLA Modules:
  0.0 370.3 jit_solution(16945968723066475624)
XLA Ops:
  7.2 0.9 copy.41
  8.1 0.1 eq.31
  8.2 0.1 eq.27
  8.3 0.1 reshape.221
  8.4 4.5 %reduce-window.6 = s32[16,8,128]{2,1,0:T(8,128)S(1)} reduce-window(s32[16,8,128]{2,1,0:T(8,128)S(1)} %fusion.34, s32[]{:T(128)} %constant.50.clone.1), window={size=1x1x128 pad=0_0x0_0x127_0}, to_apply=%region_0.0 | reduce-window | flops 2080768 | bytes 131076 | tf_op jit(solution)/shard_map/reduce-window
  12.9 0.1 slice.14
  13.0 0.1 copy.44
  13.2 0.1 add_add_fusion
  13.4 17.0 %scatter_custom_fusion = bf16[1536,1024]{1,0:T(8,128)(2,1)} fusion(s32[1024]{0:T(1024)S(1)} %bitcast.80, bf16[128,1024]{1,0:T(8,128)(2,1)} %param.7, s32[1024]{0:T(1024)S(1)} %broadcast_clamp_fusion.1, bf16[]{:T(256)} %constant.49.clone.1), kind=kCustom, calls=%fused_computation.30 | custom fusion | bytes 3146240 | tf_op jit(solution)/shard_map/scatter | solution.py:56
  30.4 4.0 %copy.46 = bf16[2,8,96,1024]{3,2,0,1:T(8,128)(2,1)} copy(bf16[2,8,96,1024]{3,2,1,0:T(8,128)(2,1)} %bitcast.75) | data formatting | bytes 6291456 | tf_op jit(solution)/shard_map/reshape | solution.py:57
  34.4 7.4 %all-to-all-start = ((bf16[2,8,96,1024]{3,2,0,1:T(8,128)(2,1)}), bf16[2,8,96,1024]{3,2,0,1:T(8,128)(2,1)}, u32[]{:S(2)}, u32[]{:S(2)}) async-start(bf16[2,8,96,1024]{3,2,0,1:T(8,128)(2,1)} %copy.46), calls=%async_computation | async-start | bytes 6291456 | tf_op jit(solution)/shard_map/all_to_all | solution.py:67
  41.9 0.1 copy.40
  42.0 0.1 mul.86
  42.1 7.8 %scatter_custom_fusion.1 = bf16[1536,1024]{1,0:T(8,128)(2,1)} fusion(s32[1024]{0:T(1024)S(1)} %bitcast.81, f32[128,1024]{1,0:T(8,128)S(1)} %convert_element_type.59, f32[1024]{0:T(1024)S(1)} %mul.86, bf16[]{:T(256)} %constant.49.clone.1), kind=kCustom, calls=%fused_computation.26 | custom fusion | flops 2097152 | bytes 3674114 | tf_op jit(solution)/shard_map/scatter | solution.py:56
  49.9 3.9 %copy.52 = bf16[2,8,96,1024]{3,2,0,1:T(8,128)(2,1)} copy(bf16[2,8,96,1024]{3,2,1,0:T(8,128)(2,1)} %bitcast.74) | data formatting | bytes 6291456 | tf_op jit(solution)/shard_map/reshape | solution.py:57
  53.9 58.8 %all-to-all-done = bf16[2,8,96,1024]{3,2,0,1:T(8,128)(2,1)} async-done(((bf16[2,8,96,1024]{3,2,0,1:T(8,128)(2,1)}), bf16[2,8,96,1024]{3,2,0,1:T(8,128)(2,1)}, u32[]{:S(2)}, u32[]{:S(2)}) %all-to-all-start) | async-done | bytes 3145760 | tf_op jit(solution)/shard_map/all_to_all | solution.py:67
  112.7 4.5 %all-to-all-start.2 = ((bf16[2,8,96,1024]{3,2,0,1:T(8,128)(2,1)}), bf16[2,8,96,1024]{3,2,0,1:T(8,128)(2,1)}, u32[]{:S(2)}, u32[]{:S(2)}) async-start(bf16[2,8,96,1024]{3,2,0,1:T(8,128)(2,1)} %copy.52), calls=%async_computation.2 | async-start | bytes 6291456 | tf_op jit(solution)/shard_map/all_to_all | solution.py:73
  117.2 5.2 %fusion.5 = f32[2,8,96,384]{3,2,1,0:T(8,128)} fusion(bf16[2,8,96,1024]{3,2,0,1:T(8,128)(2,1)} %all-to-all-done, bf16[2,1024,384]{2,1,0:T(8,128)(2,1)S(1)} %copy-done.2), kind=kOutput, calls=%fused_computation.16 | convolution fusion | flops 1207959552 | bytes 7077888 | tf_op jit(solution)/shard_map/esnd,edf->esnf/dot_general | solution.py:16
  122.4 5.1 %fusion.7 = f32[2,8,96,384]{3,2,1,0:T(8,128)} fusion(bf16[2,8,96,1024]{3,2,0,1:T(8,128)(2,1)} %all-to-all-done, bf16[2,1024,384]{2,1,0:T(8,128)(2,1)S(1)} %copy-done.3), kind=kOutput, calls=%fused_computation.18 | convolution fusion | flops 1207959552 | bytes 7077888 | tf_op jit(solution)/shard_map/esnd,edf->esnf/dot_general | solution.py:13
  127.5 59.8 %all-to-all-done.2 = bf16[2,8,96,1024]{3,2,0,1:T(8,128)(2,1)} async-done(((bf16[2,8,96,1024]{3,2,0,1:T(8,128)(2,1)}), bf16[2,8,96,1024]{3,2,0,1:T(8,128)(2,1)}, u32[]{:S(2)}, u32[]{:S(2)}) %all-to-all-start.2) | async-done | bytes 3145760 | tf_op jit(solution)/shard_map/all_to_all | solution.py:73
  187.3 7.2 %multiply_convert_fusion = (bf16[2,8,96,384]{3,2,1,0:T(8,128)(2,1)}, bf16[2,8,96,384]{3,2,1,0:T(8,128)(2,1)}, bf16[2,8,96,384]{3,2,1,0:T(8,128)(2,1)S(1)}) fusion(f32[2,8,96,384]{3,2,1,0:T(8,128)} %fusion.7, f32[2,8,96,384]{3,2,1,0:T(8,128)} %fusion.5, bf16[2,384,1024]{2,1,0:T(8,128)(2,1)S(1)} %copy-done, bf16[2,8,96,1024]{3,2,0,1:T(8,128)(2,1)} %all-to-all-done.2), kind=kOutput, calls=%fused_computation.20 | convolution fusion | flops 1216806912 | bytes 12976128 | tf_op jit(solution)/shard_map/esnd,efd->esnf/dot_general | solution.py:26
  194.5 1.8 convolution_convert_fusion
  196.3 2.1 copy.49
  198.4 4.5 %all-to-all-start.1 = ((bf16[2,8,96,1024]{3,2,0,1:T(8,128)(2,1)}), bf16[2,8,96,1024]{3,2,0,1:T(8,128)(2,1)}, u32[]{:S(2)}, u32[]{:S(2)}) async-start(bf16[2,8,96,1024]{3,2,0,1:T(8,128)(2,1)} %copy.49), calls=%async_computation.1 | async-start | bytes 6291456 | tf_op jit(solution)/shard_map/all_to_all | solution.py:71
  202.9 0.3 reduce-scatter.8.cloned.1.call-start
  203.2 4.9 %bitcast_convert_fusion = bf16[2,384,1024]{2,1,0:T(8,128)(2,1)} fusion(bf16[2,8,96,384]{3,2,1,0:T(8,128)(2,1)} %copy-done.10, bf16[2,8,96,1024]{3,2,0,1:T(8,128)(2,1)} %all-to-all-done.2), kind=kOutput, calls=%fused_computation.9 | convolution fusion | flops 1208745984 | bytes 5898240 | tf_op jit(solution)/shard_map/esnf,esnd->efd/dot_general | solution.py:78
  208.1 4.9 %bitcast_convert_fusion.1 = bf16[2,1024,384]{2,1,0:T(8,128)(2,1)} fusion(bf16[2,8,96,1024]{3,2,0,1:T(8,128)(2,1)} %all-to-all-done, bf16[2,8,96,384]{3,2,1,0:T(8,128)(2,1)S(1)} %copy-done.6), kind=kOutput, calls=%fused_computation.10 | convolution fusion | flops 1208745984 | bytes 5898240 | tf_op jit(solution)/shard_map/esnd,esnf->edf/dot_general | solution.py:82
  213.1 1.4 copy-done.4
  214.4 3.2 fusion.22
  217.7 1.8 add_convert_fusion
  219.5 1.9 copy.54
  221.4 51.6 %all-to-all-done.1 = bf16[2,8,96,1024]{3,2,0,1:T(8,128)(2,1)} async-done(((bf16[2,8,96,1024]{3,2,0,1:T(8,128)(2,1)}), bf16[2,8,96,1024]{3,2,0,1:T(8,128)(2,1)}, u32[]{:S(2)}, u32[]{:S(2)}) %all-to-all-start.1) | async-done | bytes 3145760 | tf_op jit(solution)/shard_map/all_to_all | solution.py:71
  273.1 4.5 %all-to-all-start.3 = ((bf16[2,8,96,1024]{3,2,0,1:T(8,128)(2,1)}), bf16[2,8,96,1024]{3,2,0,1:T(8,128)(2,1)}, u32[]{:S(2)}, u32[]{:S(2)}) async-start(bf16[2,8,96,1024]{3,2,0,1:T(8,128)(2,1)} %copy.54), calls=%async_computation.3 | async-start | bytes 6291456 | tf_op jit(solution)/shard_map/all_to_all | solution.py:77
  277.5 0.3 reduce-scatter.4.cloned.1.call-start
  277.8 4.9 %bitcast_convert_fusion.2 = bf16[2,1024,384]{2,1,0:T(8,128)(2,1)} fusion(bf16[2,8,96,1024]{3,2,0,1:T(8,128)(2,1)} %all-to-all-done, bf16[2,8,96,384]{3,2,1,0:T(8,128)(2,1)S(1)} %copy-done.5), kind=kOutput, calls=%fused_computation.11 | convolution fusion | flops 1208745984 | bytes 5898240 | tf_op jit(solution)/shard_map/esnd,esnf->edf/dot_general | solution.py:79
  282.8 2.0 convert_element_type.69
  284.8 1.9 convert_element_type.67
  286.7 25.3 %reduce-scatter.4.cloned.1.call-done = bf16[2,256,384]{2,1,0:T(8,128)(2,1)} async-done(((bf16[2,1024,384]{2,1,0:T(8,128)(2,1)}), bf16[2,256,384]{2,1,0:T(8,128)(2,1)}) %reduce-scatter.4.cloned.1.call-update) | async-done | bytes 393232 | tf_op jit(solution)/shard_map/reduce_scatter | solution.py:87
  312.0 1.9 convert_element_type.65
  313.9 4.0 %copy.50 = bf16[2,8,96,1024]{3,2,1,0:T(8,128)(2,1)} copy(bf16[2,8,96,1024]{3,2,0,1:T(8,128)(2,1)} %all-to-all-done.1) | data formatting | bytes 6291456 | tf_op jit(solution)/shard_map/all_to_all | solution.py:71
  317.9 8.3 %gather_fusion = bf16[1024,1024]{1,0:T(8,128)(2,1)} fusion(bf16[1536,1024]{1,0:T(8,128)(2,1)} %bitcast.73, s32[1024]{0:T(1024)S(1)} %broadcast_clamp_fusion), kind=kCustom, calls=%fused_computation.1 | custom fusion | bytes 4198400 | tf_op jit(solution)/shard_map/gather | solution.py:60
  326.2 2.8 fusion.12
  329.0 0.7 copy.63
  329.7 3.7 multiply_reduce_fusion
  333.3 14.4 %all-to-all-done.3 = bf16[2,8,96,1024]{3,2,0,1:T(8,128)(2,1)} async-done(((bf16[2,8,96,1024]{3,2,0,1:T(8,128)(2,1)}), bf16[2,8,96,1024]{3,2,0,1:T(8,128)(2,1)}, u32[]{:S(2)}, u32[]{:S(2)}) %all-to-all-start.3) | async-done | bytes 3145760 | tf_op jit(solution)/shard_map/all_to_all | solution.py:77
  347.7 4.0 %copy.55 = bf16[2,8,96,1024]{3,2,1,0:T(8,128)(2,1)} copy(bf16[2,8,96,1024]{3,2,0,1:T(8,128)(2,1)} %all-to-all-done.3) | data formatting | bytes 6291456 | tf_op jit(solution)/shard_map/all_to_all | solution.py:77
  351.7 8.4 %gather_fusion.1 = bf16[1024,1024]{1,0:T(8,128)(2,1)} fusion(bf16[1536,1024]{1,0:T(8,128)(2,1)} %bitcast.72, s32[1024]{0:T(1024)S(1)} %broadcast_clamp_fusion), kind=kCustom, calls=%fused_computation.2 | custom fusion | bytes 4198400 | tf_op jit(solution)/shard_map/gather | solution.py:60
  360.1 3.7 %bitcast_reduce_fusion = bf16[128,1024]{1,0:T(8,128)(2,1)} fusion(bf16[1024,1024]{1,0:T(8,128)(2,1)} %gather_fusion.1), kind=kLoop, calls=%fused_computation.27 | loop fusion | flops 917504 | bytes 2359296 | tf_op jit(solution)/shard_map/reduce_sum | solution.py:97
  (37 shorter events, 0.4 us)
Async XLA Ops:
  7.2 180.1 %copy-start = (bf16[2,384,1024]{2,1,0:T(8,128)(2,1)S(1)}, bf16[2,384,1024]{2,1,0:T(8,128)(2,1)}, u32[]{:S(2)}) copy-start(bf16[2,384,1024]{2,1,0:T(8,128)(2,1)} %param.13) | copy-start | bytes 4718596
  34.4 7.4 %copy-start.9 = (f32[128,8]{0,1:T(8,128)S(1)}, f32[128,8]{0,1:T(8,128)}, u32[]{:S(2)}) copy-start(f32[128,8]{0,1:T(8,128)} %param.9) | copy-start | bytes 12292
  34.4 7.6 %copy-start.8 = (bf16[128,1024]{1,0:T(8,128)(2,1)S(1)}, bf16[128,1024]{1,0:T(8,128)(2,1)}, u32[]{:S(2)}) copy-start(bf16[128,1024]{1,0:T(8,128)(2,1)} %param.10) | copy-start | bytes 786436
  34.4 78.2 %all-to-all-start = ((bf16[2,8,96,1024]{3,2,0,1:T(8,128)(2,1)}), bf16[2,8,96,1024]{3,2,0,1:T(8,128)(2,1)}, u32[]{:S(2)}, u32[]{:S(2)}) async-start(bf16[2,8,96,1024]{3,2,0,1:T(8,128)(2,1)} %copy.46), calls=%async_computation | async-start | bytes 6291456 | tf_op jit(solution)/shard_map/all_to_all | solution.py:67
  53.9 63.3 %copy-start.2 = (bf16[2,1024,384]{2,1,0:T(8,128)(2,1)S(1)}, bf16[2,1024,384]{2,1,0:T(8,128)(2,1)}, u32[]{:S(2)}) copy-start(bf16[2,1024,384]{2,1,0:T(8,128)(2,1)} %param.12) | copy-start | bytes 4718596
  112.7 74.6 %all-to-all-start.2 = ((bf16[2,8,96,1024]{3,2,0,1:T(8,128)(2,1)}), bf16[2,8,96,1024]{3,2,0,1:T(8,128)(2,1)}, u32[]{:S(2)}, u32[]{:S(2)}) async-start(bf16[2,8,96,1024]{3,2,0,1:T(8,128)(2,1)} %copy.52), calls=%async_computation.2 | async-start | bytes 6291456 | tf_op jit(solution)/shard_map/all_to_all | solution.py:73
  117.1 5.2 %copy-start.3 = (bf16[2,1024,384]{2,1,0:T(8,128)(2,1)S(1)}, bf16[2,1024,384]{2,1,0:T(8,128)(2,1)}, u32[]{:S(2)}) copy-start(bf16[2,1024,384]{2,1,0:T(8,128)(2,1)} %param.11) | copy-start | bytes 4718596
  194.5 1.8 copy-start.10
  198.4 74.6 %all-to-all-start.1 = ((bf16[2,8,96,1024]{3,2,0,1:T(8,128)(2,1)}), bf16[2,8,96,1024]{3,2,0,1:T(8,128)(2,1)}, u32[]{:S(2)}, u32[]{:S(2)}) async-start(bf16[2,8,96,1024]{3,2,0,1:T(8,128)(2,1)} %copy.49), calls=%async_computation.1 | async-start | bytes 6291456 | tf_op jit(solution)/shard_map/all_to_all | solution.py:71
  202.9 5.2 %copy-start.6 = (bf16[2,8,96,384]{3,2,1,0:T(8,128)(2,1)S(1)}, bf16[2,8,96,384]{3,2,1,0:T(8,128)(2,1)}, u32[]{:S(2)}) copy-start(bf16[2,8,96,384]{3,2,1,0:T(8,128)(2,1)} %get-tuple-element.6) | copy-start | bytes 3538948
  202.9 79.9 %reduce-scatter.8.cloned.1.call-start = ((), (), s32[]{:S(2)}) async-start(), calls=%async_computation.9 | async-start | bytes 1966080 | tf_op jit(solution)/shard_map/reduce_scatter | solution.py:83
  208.1 76.7 %reduce-scatter.6.cloned.1.call-start = ((), (), s32[]{:S(2)}) async-start(), calls=%async_computation.8 | async-start | bytes 1966080 | tf_op jit(solution)/shard_map/reduce_scatter | solution.py:90
  213.0 1.4 copy-start.4
  214.4 3.2 copy-start.7
  221.4 56.4 %copy-start.5 = (bf16[2,8,96,384]{3,2,1,0:T(8,128)(2,1)S(1)}, bf16[2,8,96,384]{3,2,1,0:T(8,128)(2,1)}, u32[]{:S(2)}) copy-start(bf16[2,8,96,384]{3,2,1,0:T(8,128)(2,1)} %get-tuple-element.7) | copy-start | bytes 3538948
  273.1 74.6 %all-to-all-start.3 = ((bf16[2,8,96,1024]{3,2,0,1:T(8,128)(2,1)}), bf16[2,8,96,1024]{3,2,0,1:T(8,128)(2,1)}, u32[]{:S(2)}, u32[]{:S(2)}) async-start(bf16[2,8,96,1024]{3,2,0,1:T(8,128)(2,1)} %copy.54), calls=%async_computation.3 | async-start | bytes 6291456 | tf_op jit(solution)/shard_map/all_to_all | solution.py:77
  277.5 34.5 %reduce-scatter.4.cloned.1.call-start = ((), (), s32[]{:S(2)}) async-start(), calls=%async_computation.7 | async-start | bytes 1966080 | tf_op jit(solution)/shard_map/reduce_scatter | solution.py:87
  351.6 12.2 %copy-start.1 = (bf16[2,384,1024]{2,1,0:T(8,128)(2,1)S(1)}, bf16[2,384,1024]{2,1,0:T(8,128)(2,1)}, u32[]{:S(2)}) copy-start(bf16[2,384,1024]{2,1,0:T(8,128)(2,1)} %param.13) | copy-start | bytes 4718596
Sparse Core Ops, SparseCore 0:
  208.2 29.1 reduce-scatter.7
  239.9 28.0 reduce-scatter.5
  282.9 29.0 reduce-scatter.3
where the time goes:
time: 372 us; the launch traced here: 370 us
  waiting for transfers between devices  210 us (56%)
  local copies, waits for them, and re-layouts  57.4 us (15%)
  matrix products  41.9 us (11%)
  other arithmetic  25.8 us (7%)
  starting transfers between devices  21.4 us (6%)
  between operations  14 us (4%)
    all_to_all x1, waiting for transfers between devices, per_device(): lax.all_to_all(sent_grads, 'ep', split_axis=1, concat_axis=1, tiled=True)  59.8 us
    all_to_all x1, waiting for transfers between devices, per_device(): lax.all_to_all(sent_tokens, 'ep', split_axis=1, concat_axis=1, tiled=True)  58.8 us
    all_to_all x1, waiting for transfers between devices, per_device(): lax.all_to_all(expert_out, 'ep', split_axis=1, concat_axis=1, tiled=True)  51.6 us
    reduce_scatter x1, waiting for transfers between devices, per_device(): lax.psum_scatter(grad_gate.astype(jnp.bfloat16), 'rep', scatter_dimension...  25.3 us
    scatter x1, local copies, waits for them, and re-layouts, pack_rows(): jnp.zeros((slot_total, model_width), jnp.bfloat16).at[target].set(pair_rows)  17 us
    gather x2, local copies, waits for them, and re-layouts, unpack_rows(): returned.reshape(slot_total, model_width)[target]  16.7 us
    all_to_all x1, waiting for transfers between devices, per_device(): lax.all_to_all(in_grads, 'ep', split_axis=1, concat_axis=1, tiled=True)  14.4 us
    reshape x2, local copies, waits for them, and re-layouts, pack_rows(): return filled.reshape(local_experts, peer_count, capacity, model_width)  7.93 us
  transfers between devices with their start and end apart: 7, of which 5 were waited for; matrix products, arithmetic and copies ran while one was open for 19% of the time, Pallas kernels for 0%

commit v1 on v0

--- a/solution.py
+++ b/solution.py
@@ -74,7 +74,9 @@
     gate_delta, up_delta, in_grads = expert_backward(
         out_rows, gate_pre, up_pre, gate_weight, up_weight, down_weight
     )
-    in_returned = lax.all_to_all(in_grads, "ep", split_axis=1, concat_axis=1, tiled=True)
+    parts = jnp.split(in_grads, lax.axis_size("ep"), axis=1)
+    got = lax.all_to_all(jnp.stack(parts), "ep", 0, 0)
+    in_returned = jnp.concatenate(got, axis=1)
     grad_down = jnp.einsum("esnf,esnd->efd", hidden, out_rows, preferred_element_type=jnp.float32)
     grad_gate = jnp.einsum(
         "esnd,esnf->edf", expert_in, gate_delta, preferred_element_type=jnp.float32

time: 372 us -> 378 us (1.016)
  local copies, waits for them, and re-layouts: 57.4 us -> 62.8 us
    unnamed x24 -> x31, local copies, waits for them, and re-layouts: 2.44 us -> 9.11 us
    all_to_all x1 -> x0, local copies, waits for them, and re-layouts: 3.96 us -> none  [per_device(): lax.all_to_all(in_grads, 'ep', split_axis=1, concat_axis=1, tiled=True)]
    reshape x0 -> x1, local copies, waits for them, and re-layouts: none -> 3.96 us  [per_device(): in_returned = jnp.concatenate(got, axis=1)]
  transfers between devices with their start and end apart: 7 -> 7, of which waited for: 5 -> 5; matrix products, arithmetic and copies ran while one was open for 19% -> 20% of each run, Pallas kernels for 0% -> 0%
where the time goes in v1:
time: 378 us; the launch traced here: 377 us
  waiting for transfers between devices  210 us (56%)
  local copies, waits for them, and re-layouts  62.8 us (17%)
  matrix products  42.7 us (11%)
  other arithmetic  25.7 us (7%)
  starting transfers between devices  21.8 us (6%)
  between operations  13.9 us (4%)
    all_to_all x1, waiting for transfers between devices, per_device(): lax.all_to_all(sent_grads, 'ep', split_axis=1, concat_axis=1, tiled=True)  59.5 us
    all_to_all x1, waiting for transfers between devices, per_device(): lax.all_to_all(sent_tokens, 'ep', split_axis=1, concat_axis=1, tiled=True)  58.8 us
    all_to_all x1, waiting for transfers between devices, per_device(): lax.all_to_all(expert_out, 'ep', split_axis=1, concat_axis=1, tiled=True)  52.1 us
    reduce_scatter x1, waiting for transfers between devices, per_device(): lax.psum_scatter(grad_gate.astype(jnp.bfloat16), 'rep', scatter_dimension...  25.3 us
    scatter x1, local copies, waits for them, and re-layouts, pack_rows(): jnp.zeros((slot_total, model_width), jnp.bfloat16).at[target].set(pair_rows)  16.8 us
    gather x2, local copies, waits for them, and re-layouts, unpack_rows(): returned.reshape(slot_total, model_width)[target]  16.7 us
    all_to_all x1, waiting for transfers between devices, per_device(): got = lax.all_to_all(jnp.stack(parts), 'ep', 0, 0)  14.4 us
    unnamed x31, local copies, waits for them, and re-layouts  9.11 us
  transfers between devices with their start and end apart: 7, of which 5 were waited for; matrix products, arithmetic and copies ran while one was open for 20% of the time, Pallas kernels for 0%

profile of v1, /device:TPU:0, one launch (start us, length us, event | category | flops | bytes accessed | tf_op | source)
XLA Modules:
  0.0 377.1 jit_solution(9531456855052737407)
XLA Ops:
  7.2 0.9 copy.62
  8.4 4.5 %reduce-window.6 = s32[16,8,128]{2,1,0:T(8,128)S(1)} reduce-window(s32[16,8,128]{2,1,0:T(8,128)S(1)} %fusion.42, s32[]{:T(128)} %constant.50.clone.1), window={size=1x1x128 pad=0_0x0_0x127_0}, to_apply=%region_0.0 | reduce-window | flops 2080768 | bytes 131076 | tf_op jit(solution)/shard_map/reduce-window
  13.4 16.8 %scatter_custom_fusion = bf16[1536,1024]{1,0:T(8,128)(2,1)} fusion(s32[1024]{0:T(1024)S(1)} %bitcast.127, bf16[128,1024]{1,0:T(8,128)(2,1)} %param.7, s32[1024]{0:T(1024)S(1)} %broadcast_clamp_fusion.1, bf16[]{:T(256)} %constant.49.clone.1), kind=kCustom, calls=%fused_computation.30 | custom fusion | bytes 3146240 | tf_op jit(solution)/shard_map/scatter | solution.py:56
  30.2 4.0 %copy.67 = bf16[2,8,96,1024]{3,2,0,1:T(8,128)(2,1)} copy(bf16[2,8,96,1024]{3,2,1,0:T(8,128)(2,1)} %bitcast.122) | data formatting | bytes 6291456 | tf_op jit(solution)/shard_map/reshape | solution.py:57
  34.2 7.4 %all-to-all-start = ((bf16[2,8,96,1024]{3,2,0,1:T(8,128)(2,1)}), bf16[2,8,96,1024]{3,2,0,1:T(8,128)(2,1)}, u32[]{:S(2)}, u32[]{:S(2)}) async-start(bf16[2,8,96,1024]{3,2,0,1:T(8,128)(2,1)} %copy.67), calls=%async_computation | async-start | bytes 6291456 | tf_op jit(solution)/shard_map/all_to_all | solution.py:67
  41.9 7.8 %scatter_custom_fusion.1 = bf16[1536,1024]{1,0:T(8,128)(2,1)} fusion(s32[1024]{0:T(1024)S(1)} %bitcast.128, f32[128,1024]{1,0:T(8,128)S(1)} %convert_element_type.59, f32[1024]{0:T(1024)S(1)} %mul.86, bf16[]{:T(256)} %constant.49.clone.1), kind=kCustom, calls=%fused_computation.26 | custom fusion | flops 2097152 | bytes 3674114 | tf_op jit(solution)/shard_map/scatter | solution.py:56
  49.6 4.0 %copy.73 = bf16[2,8,96,1024]{3,2,0,1:T(8,128)(2,1)} copy(bf16[2,8,96,1024]{3,2,1,0:T(8,128)(2,1)} %bitcast.121) | data formatting | bytes 6291456 | tf_op jit(solution)/shard_map/reshape | solution.py:57
  53.6 58.8 %all-to-all-done = bf16[2,8,96,1024]{3,2,0,1:T(8,128)(2,1)} async-done(((bf16[2,8,96,1024]{3,2,0,1:T(8,128)(2,1)}), bf16[2,8,96,1024]{3,2,0,1:T(8,128)(2,1)}, u32[]{:S(2)}, u32[]{:S(2)}) %all-to-all-start) | async-done | bytes 3145760 | tf_op jit(solution)/shard_map/all_to_all | solution.py:67
  112.4 4.5 %all-to-all-start.2 = ((bf16[2,8,96,1024]{3,2,0,1:T(8,128)(2,1)}), bf16[2,8,96,1024]{3,2,0,1:T(8,128)(2,1)}, u32[]{:S(2)}, u32[]{:S(2)}) async-start(bf16[2,8,96,1024]{3,2,0,1:T(8,128)(2,1)} %copy.73), calls=%async_computation.2 | async-start | bytes 6291456 | tf_op jit(solution)/shard_map/all_to_all | solution.py:73
  117.2 5.3 %fusion.5 = f32[2,8,96,384]{3,2,1,0:T(8,128)} fusion(bf16[2,8,96,1024]{3,2,0,1:T(8,128)(2,1)} %all-to-all-done, bf16[2,1024,384]{2,1,0:T(8,128)(2,1)S(1)} %copy-done.2), kind=kOutput, calls=%fused_computation.16 | convolution fusion | flops 1207959552 | bytes 7077888 | tf_op jit(solution)/shard_map/esnd,edf->esnf/dot_general | solution.py:16
  122.5 5.1 %fusion.7 = f32[2,8,96,384]{3,2,1,0:T(8,128)} fusion(bf16[2,8,96,1024]{3,2,0,1:T(8,128)(2,1)} %all-to-all-done, bf16[2,1024,384]{2,1,0:T(8,128)(2,1)S(1)} %copy-done.3), kind=kOutput, calls=%fused_computation.18 | convolution fusion | flops 1207959552 | bytes 7077888 | tf_op jit(solution)/shard_map/esnd,edf->esnf/dot_general | solution.py:13
  127.6 59.5 %all-to-all-done.2 = bf16[2,8,96,1024]{3,2,0,1:T(8,128)(2,1)} async-done(((bf16[2,8,96,1024]{3,2,0,1:T(8,128)(2,1)}), bf16[2,8,96,1024]{3,2,0,1:T(8,128)(2,1)}, u32[]{:S(2)}, u32[]{:S(2)}) %all-to-all-start.2) | async-done | bytes 3145760 | tf_op jit(solution)/shard_map/all_to_all | solution.py:73
  187.1 7.2 %multiply_convert_fusion = (bf16[2,8,96,384]{3,2,1,0:T(8,128)(2,1)}, bf16[2,8,96,384]{3,2,1,0:T(8,128)(2,1)}, bf16[2,8,96,384]{3,2,1,0:T(8,128)(2,1)S(1)}) fusion(f32[2,8,96,384]{3,2,1,0:T(8,128)} %fusion.7, f32[2,8,96,384]{3,2,1,0:T(8,128)} %fusion.5, bf16[2,384,1024]{2,1,0:T(8,128)(2,1)S(1)} %copy-done, bf16[2,8,96,1024]{3,2,0,1:T(8,128)(2,1)} %all-to-all-done.2), kind=kOutput, calls=%fused_computation.20 | convolution fusion | flops 1216806912 | bytes 12976128 | tf_op jit(solution)/shard_map/esnd,efd->esnf/dot_general | solution.py:26
  194.2 1.0 copy-done.10
  195.3 4.5 %bitcast_convert_fusion = bf16[2,384,1024]{2,1,0:T(8,128)(2,1)} fusion(bf16[2,8,96,384]{3,2,1,0:T(8,128)(2,1)S(1)} %get-tuple-element.8, bf16[2,8,96,1024]{3,2,0,1:T(8,128)(2,1)} %all-to-all-done.2), kind=kOutput, calls=%fused_computation.9 | convolution fusion | flops 1208745984 | bytes 5898240 | tf_op jit(solution)/shard_map/esnf,esnd->efd/dot_general | solution.py:80
  199.8 3.1 convolution_convert_fusion
  202.9 2.1 copy.70
  205.0 4.6 %all-to-all-start.1 = ((bf16[2,8,96,1024]{3,2,0,1:T(8,128)(2,1)}), bf16[2,8,96,1024]{3,2,0,1:T(8,128)(2,1)}, u32[]{:S(2)}, u32[]{:S(2)}) async-start(bf16[2,8,96,1024]{3,2,0,1:T(8,128)(2,1)} %copy.70), calls=%async_computation.1 | async-start | bytes 6291456 | tf_op jit(solution)/shard_map/all_to_all | solution.py:71
  209.6 0.3 reduce-scatter.6.cloned.1.call-start
  209.9 4.9 %bitcast_convert_fusion.1 = bf16[2,1024,384]{2,1,0:T(8,128)(2,1)} fusion(bf16[2,8,96,1024]{3,2,0,1:T(8,128)(2,1)} %all-to-all-done, bf16[2,8,96,384]{3,2,1,0:T(8,128)(2,1)S(1)} %copy-done.6), kind=kOutput, calls=%fused_computation.10 | convolution fusion | flops 1208745984 | bytes 5898240 | tf_op jit(solution)/shard_map/esnd,esnf->edf/dot_general | solution.py:84
  214.8 1.6 copy-done.4
  216.4 3.2 fusion.22
  219.6 1.8 add_convert_fusion
  221.4 0.8 fusion.39
  222.2 0.8 fusion.38
  223.0 0.8 fusion.37
  223.8 0.8 fusion.36
  224.6 0.8 fusion.35
  225.4 0.8 fusion.34
  226.1 0.8 fusion.33
  226.9 0.8 fusion.32
  227.7 52.1 %all-to-all-done.1 = bf16[2,8,96,1024]{3,2,0,1:T(8,128)(2,1)} async-done(((bf16[2,8,96,1024]{3,2,0,1:T(8,128)(2,1)}), bf16[2,8,96,1024]{3,2,0,1:T(8,128)(2,1)}, u32[]{:S(2)}, u32[]{:S(2)}) %all-to-all-start.1) | async-done | bytes 3145760 | tf_op jit(solution)/shard_map/all_to_all | solution.py:71
  279.8 4.5 %all-to-all-start.3 = ((bf16[8,2,1,96,1024]{4,3,1,2,0:T(8,128)(2,1)}), bf16[8,2,1,96,1024]{4,3,1,2,0:T(8,128)(2,1)}, u32[]{:S(2)}, u32[]{:S(2)}) async-start(bf16[8,2,1,96,1024]{4,3,1,2,0:T(8,128)(2,1)} %fusion.32), calls=%async_computation.3 | async-start | bytes 6291456 | tf_op jit(solution)/shard_map/all_to_all | solution.py:78
  284.2 0.3 reduce-scatter.4.cloned.1.call-start
  284.6 4.9 %bitcast_convert_fusion.2 = bf16[2,1024,384]{2,1,0:T(8,128)(2,1)} fusion(bf16[2,8,96,1024]{3,2,0,1:T(8,128)(2,1)} %all-to-all-done, bf16[2,8,96,384]{3,2,1,0:T(8,128)(2,1)S(1)} %copy-done.5), kind=kOutput, calls=%fused_computation.11 | convolution fusion | flops 1208745984 | bytes 5898240 | tf_op jit(solution)/shard_map/esnd,esnf->edf/dot_general | solution.py:81
  289.5 2.0 convert_element_type.69
  291.5 1.9 convert_element_type.67
  293.4 25.3 %reduce-scatter.4.cloned.1.call-done = bf16[2,256,384]{2,1,0:T(8,128)(2,1)} async-done(((bf16[2,1024,384]{2,1,0:T(8,128)(2,1)}), bf16[2,256,384]{2,1,0:T(8,128)(2,1)}) %reduce-scatter.4.cloned.1.call-update) | async-done | bytes 393232 | tf_op jit(solution)/shard_map/reduce_scatter | solution.py:89
  318.7 1.9 convert_element_type.65
  320.6 4.0 %copy.71 = bf16[2,8,96,1024]{3,2,1,0:T(8,128)(2,1)} copy(bf16[2,8,96,1024]{3,2,0,1:T(8,128)(2,1)} %all-to-all-done.1) | data formatting | bytes 6291456 | tf_op jit(solution)/shard_map/all_to_all | solution.py:71
  324.6 8.3 %gather_fusion = bf16[1024,1024]{1,0:T(8,128)(2,1)} fusion(bf16[1536,1024]{1,0:T(8,128)(2,1)} %bitcast.120, s32[1024]{0:T(1024)S(1)} %broadcast_clamp_fusion), kind=kCustom, calls=%fused_computation.1 | custom fusion | bytes 4198400 | tf_op jit(solution)/shard_map/gather | solution.py:60
  332.9 2.8 fusion.12
  335.7 0.7 copy.90
  336.4 3.7 multiply_reduce_fusion
  340.1 14.4 %all-to-all-done.3 = bf16[8,2,1,96,1024]{4,3,1,2,0:T(8,128)(2,1)} async-done(((bf16[8,2,1,96,1024]{4,3,1,2,0:T(8,128)(2,1)}), bf16[8,2,1,96,1024]{4,3,1,2,0:T(8,128)(2,1)}, u32[]{:S(2)}, u32[]{:S(2)}) %all-to-all-start.3) | async-done | bytes 3145760 | tf_op jit(solution)/shard_map/all_to_all | solution.py:78
  354.4 4.0 %copy.82 = bf16[2,8,1,96,1024]{4,3,1,0,2:T(8,128)(2,1)} copy(bf16[2,8,1,96,1024]{4,3,0,2,1:T(8,128)(2,1)} %bitcast.27) | data formatting | bytes 6291456 | tf_op jit(solution)/shard_map/reshape | solution.py:79
  358.4 8.4 %gather_fusion.1 = bf16[1024,1024]{1,0:T(8,128)(2,1)} fusion(bf16[1536,1024]{1,0:T(8,128)(2,1)} %bitcast.119, s32[1024]{0:T(1024)S(1)} %broadcast_clamp_fusion), kind=kCustom, calls=%fused_computation.2 | custom fusion | bytes 4198400 | tf_op jit(solution)/shard_map/gather | solution.py:60
  366.8 3.7 bitcast_reduce_fusion
  (44 shorter events, 1.4 us)
Async XLA Ops:
  7.2 179.9 %copy-start = (bf16[2,384,1024]{2,1,0:T(8,128)(2,1)S(1)}, bf16[2,384,1024]{2,1,0:T(8,128)(2,1)}, u32[]{:S(2)}) copy-start(bf16[2,384,1024]{2,1,0:T(8,128)(2,1)} %param.13) | copy-start | bytes 4718596
  34.2 7.4 %copy-start.9 = (f32[128,8]{0,1:T(8,128)S(1)}, f32[128,8]{0,1:T(8,128)}, u32[]{:S(2)}) copy-start(f32[128,8]{0,1:T(8,128)} %param.9) | copy-start | bytes 12292
  34.2 7.6 %copy-start.8 = (bf16[128,1024]{1,0:T(8,128)(2,1)S(1)}, bf16[128,1024]{1,0:T(8,128)(2,1)}, u32[]{:S(2)}) copy-start(bf16[128,1024]{1,0:T(8,128)(2,1)} %param.10) | copy-start | bytes 786436
  34.2 78.2 %all-to-all-start = ((bf16[2,8,96,1024]{3,2,0,1:T(8,128)(2,1)}), bf16[2,8,96,1024]{3,2,0,1:T(8,128)(2,1)}, u32[]{:S(2)}, u32[]{:S(2)}) async-start(bf16[2,8,96,1024]{3,2,0,1:T(8,128)(2,1)} %copy.67), calls=%async_computation | async-start | bytes 6291456 | tf_op jit(solution)/shard_map/all_to_all | solution.py:67
  53.6 63.5 %copy-start.2 = (bf16[2,1024,384]{2,1,0:T(8,128)(2,1)S(1)}, bf16[2,1024,384]{2,1,0:T(8,128)(2,1)}, u32[]{:S(2)}) copy-start(bf16[2,1024,384]{2,1,0:T(8,128)(2,1)} %param.12) | copy-start | bytes 4718596
  112.4 74.6 %all-to-all-start.2 = ((bf16[2,8,96,1024]{3,2,0,1:T(8,128)(2,1)}), bf16[2,8,96,1024]{3,2,0,1:T(8,128)(2,1)}, u32[]{:S(2)}, u32[]{:S(2)}) async-start(bf16[2,8,96,1024]{3,2,0,1:T(8,128)(2,1)} %copy.73), calls=%async_computation.2 | async-start | bytes 6291456 | tf_op jit(solution)/shard_map/all_to_all | solution.py:73
  116.9 172.6 %reduce-scatter.8.cloned.1.call-start = ((), (), s32[]{:S(2)}) async-start(), calls=%async_computation.9 | async-start | bytes 1966080 | tf_op jit(solution)/shard_map/reduce_scatter | solution.py:85
  117.2 5.3 %copy-start.3 = (bf16[2,1024,384]{2,1,0:T(8,128)(2,1)S(1)}, bf16[2,1024,384]{2,1,0:T(8,128)(2,1)}, u32[]{:S(2)}) copy-start(bf16[2,1024,384]{2,1,0:T(8,128)(2,1)} %param.11) | copy-start | bytes 4718596
  194.2 1.0 copy-start.10
  205.0 4.9 %copy-start.6 = (bf16[2,8,96,384]{3,2,1,0:T(8,128)(2,1)S(1)}, bf16[2,8,96,384]{3,2,1,0:T(8,128)(2,1)}, u32[]{:S(2)}) copy-start(bf16[2,8,96,384]{3,2,1,0:T(8,128)(2,1)} %get-tuple-element.6) | copy-start | bytes 3538948
  205.0 74.8 %all-to-all-start.1 = ((bf16[2,8,96,1024]{3,2,0,1:T(8,128)(2,1)}), bf16[2,8,96,1024]{3,2,0,1:T(8,128)(2,1)}, u32[]{:S(2)}, u32[]{:S(2)}) async-start(bf16[2,8,96,1024]{3,2,0,1:T(8,128)(2,1)} %copy.70), calls=%async_computation.1 | async-start | bytes 6291456 | tf_op jit(solution)/shard_map/all_to_all | solution.py:71
  209.6 81.9 %reduce-scatter.6.cloned.1.call-start = ((), (), s32[]{:S(2)}) async-start(), calls=%async_computation.8 | async-start | bytes 1966080 | tf_op jit(solution)/shard_map/reduce_scatter | solution.py:92
  214.8 1.6 copy-start.4
  216.4 3.2 copy-start.7
  227.7 56.9 %copy-start.5 = (bf16[2,8,96,384]{3,2,1,0:T(8,128)(2,1)S(1)}, bf16[2,8,96,384]{3,2,1,0:T(8,128)(2,1)}, u32[]{:S(2)}) copy-start(bf16[2,8,96,384]{3,2,1,0:T(8,128)(2,1)} %get-tuple-element.7) | copy-start | bytes 3538948
  279.8 74.6 %all-to-all-start.3 = ((bf16[8,2,1,96,1024]{4,3,1,2,0:T(8,128)(2,1)}), bf16[8,2,1,96,1024]{4,3,1,2,0:T(8,128)(2,1)}, u32[]{:S(2)}, u32[]{:S(2)}) async-start(bf16[8,2,1,96,1024]{4,3,1,2,0:T(8,128)(2,1)} %fusion.32), calls=%async_computation.3 | async-start | bytes 6291456 | tf_op jit(solution)/shard_map/all_to_all | solution.py:78
  284.2 34.5 %reduce-scatter.4.cloned.1.call-start = ((), (), s32[]{:S(2)}) async-start(), calls=%async_computation.7 | async-start | bytes 1966080 | tf_op jit(solution)/shard_map/reduce_scatter | solution.py:89
  358.4 12.2 %copy-start.1 = (bf16[2,384,1024]{2,1,0:T(8,128)(2,1)S(1)}, bf16[2,384,1024]{2,1,0:T(8,128)(2,1)}, u32[]{:S(2)}) copy-start(bf16[2,384,1024]{2,1,0:T(8,128)(2,1)} %param.13) | copy-start | bytes 4718596
Sparse Core Ops, SparseCore 0:
  199.9 27.0 reduce-scatter.7
  229.6 27.9 reduce-scatter.5
  289.6 29.0 reduce-scatter.3
